TPU v7x, 256 devices: a whole 4x4x8 slice. The times are simulated.
256 devices in a mesh: group: 32 (over y, z), inner: 8 (over x, core).
Axes of the slice: x: 4, y: 4, z: 8, core: 2. Of those that a mesh axis runs over, the one named last changes fastest.
Arguments:
- tokens: bfloat16 [4096, 7168], P('group', 'inner'), may hold values from -6 to 6
- routes: int32 [4096, 4], P('group'), may hold values from 0 to 31, all different within a row; in each aligned block of 128 rows (0 to 127, 128 to 255, ...) at most 24 rows name the same one
- gate_weights: float32 [4096, 4], P('group'), may hold values from 0.1 to 1
- w_gate: bfloat16 [32, 7168, 2048], P('group', None, 'inner'), may hold values from -0.0625 to 0.0625
- w_up: bfloat16 [32, 7168, 2048], P('group', None, 'inner'), may hold values from -0.0625 to 0.0625
- w_down: bfloat16 [32, 2048, 7168], P('group', 'inner'), may hold values from -0.125 to 0.125
Outputs:
- moe_out: bfloat16 [4096, 7168], P('group', 'inner')
Inputs may be any that keep to these rules, and one draw needn't show every extreme that they name: `routes`: each row names 4 different expert groups. Within each aligned block of 128 rows (the rows of one index of group) no group is named by more than 24 rows, and in some blocks one group is named by exactly 24 rows.
All inputs are finite; a program needn't handle non-finite values.
Results may differ from a plain program's by a relative error of at most 0.014.
Values may be sent and summed in bfloat16 or wider, within the bound.
A program may use at most 128 MiB of HBM per device.

v0:
```python
import jax
import jax.numpy as jnp
from jax import lax
from jax.sharding import PartitionSpec as P


def layout(routes, groups, capacity):
    group_ids = jnp.arange(groups, dtype=jnp.int32)
    onehot = routes[:, :, None] == group_ids[None, None, :]
    chosen = jnp.sum(onehot.astype(jnp.int32), axis=1)
    slot_of = jnp.cumsum(chosen, axis=0) - 1
    slot_ids = jnp.arange(capacity, dtype=jnp.int32)
    placing = (chosen.T[:, None, :] == 1) & (slot_of.T[:, None, :] == slot_ids[None, :, None])
    pick_slot = jnp.take_along_axis(slot_of, routes, axis=1)
    pick_index = routes * capacity + pick_slot
    return (placing, pick_index)


def pack_rows(placing, token_rows):
    packed = jnp.einsum(
        "hct,td->hcd", placing.astype(jnp.bfloat16), token_rows, preferred_element_type=jnp.float32
    )
    return packed.astype(jnp.bfloat16)


def combine(pick_index, gate_weights, returned):
    flat_rows = returned.reshape(returned.shape[0] * returned.shape[1], returned.shape[2])
    taken = jnp.take(flat_rows, pick_index, axis=0).astype(jnp.float32)
    return jnp.sum(taken * gate_weights[:, :, None], axis=1)


def local(tokens, routes, gate_weights, w_gate, w_up, w_down):
    groups = lax.axis_size("group")
    shard_rows = tokens.shape[0]
    capacity = shard_rows * routes.shape[1] * 3 // (2 * groups)
    placing, pick_index = layout(routes, groups, capacity)
    gate_mat = w_gate[0]
    up_mat = w_up[0]
    down_mat = w_down[0]
    arrived = lax.all_to_all(
        pack_rows(placing, tokens), "group", split_axis=0, concat_axis=0, tiled=True
    )
    feature_part = lax.all_gather(arrived, "inner", axis=2, tiled=True)
    gate_add = jnp.einsum("hck,kf->hcf", feature_part, gate_mat, preferred_element_type=jnp.float32)
    up_add = jnp.einsum("hck,kf->hcf", feature_part, up_mat, preferred_element_type=jnp.float32)
    hidden = (jax.nn.silu(gate_add) * up_add).astype(jnp.bfloat16)
    partial_value = jnp.einsum(
        "hcf,fd->hcd", hidden, down_mat, preferred_element_type=jnp.float32
    ).astype(jnp.bfloat16)
    summed = lax.psum_scatter(partial_value, "inner", scatter_dimension=2, tiled=True)
    returned = lax.all_to_all(summed, "group", split_axis=0, concat_axis=0, tiled=True)
    return combine(pick_index, gate_weights, returned).astype(jnp.bfloat16)


def solution(mesh):
    placed = (
        P("group", "inner"),
        P("group", None),
        P("group", None),
        P("group", None, "inner"),
        P("group", None, "inner"),
        P("group", "inner", None),
    )
    return jax.shard_map(
        local, mesh=mesh, in_specs=placed, out_specs=P("group", "inner"), check_vma=False
    )
```

profile of v0, /device:TPU:32, one launch (start us, length us, event | category | flops | bytes accessed | tf_op | source)
XLA Modules:
  0.0 412.8 jit_solution(16734024208027349280)
XLA Ops:
  6.5 0.0 copy-start
  6.5 0.0 all-gather.2.cloned.1.call-start
  6.5 0.7 convert_reduce_fusion
  7.3 0.1 copy.44
  7.4 0.2 reduce_window_sum.11
  7.6 0.1 copy.48
  7.6 0.0 copy-done
  7.6 0.5 convolution_convert_fusion.1
  8.2 47.4 %all_to_all.10 = bf16[32,24,896]{2,1,0:T(8,128)(2,1)} all-to-all(bf16[32,24,896]{2,1,0:T(8,128)(2,1)S(1)} %convolution_convert_fusion.1), channel_id=1, replica_groups=mesh['group'=32,'inner'=8] {'group'}, dimensions={0} | all-to-all | bytes 2752512 | tf_op jit(solution)/shard_map/all_to_all | solution.py:40
  55.6 0.0 all-gather.2.cloned.1.call-update
  55.6 0.0 reduce-scatter.4.cloned.1.call-start
  55.6 59.1 %all-gather.2.cloned.1.call-done = bf16[32,24,7168]{2,1,0:T(8,128)(2,1)} async-done(((bf16[32,24,896]{2,1,0:T(8,128)(2,1)}), bf16[32,24,7168]{2,1,0:T(8,128)(2,1)}) %all-gather.2.cloned.1.call-update) | async-done | bytes 11010064 | tf_op jit(solution)/shard_map/all_gather | solution.py:43
  114.7 0.0 copy-start.5
  114.7 0.0 copy-start.6
  114.7 7.0 %fusion.3 = f32[32,24,256]{2,1,0:T(8,128)S(1)} fusion(bf16[32,24,7168]{2,1,0:T(8,128)(2,1)} %all-gather.2.cloned.1.call-done, bf16[1,7168,256]{2,1,0:T(8,128)(2,1)} %param.9), kind=kOutput, calls=%fused_computation.6 | convolution fusion | flops 2818572288 | bytes 15466496 | tf_op jit(solution)/shard_map/hck,kf->hcf/dot_general | solution.py:44
  121.8 1.3 copy-done.5
  123.1 1.0 copy-done.6
  124.1 0.0 copy-start.2
  124.1 3.2 fusion.8
  127.4 0.0 copy-done.2
  127.4 5.8 %convolution_convert_fusion = bf16[32,24,7168]{2,1,0:T(8,128)(2,1)} fusion(bf16[32,24,256]{2,1,0:T(8,128)(2,1)S(1)} %fusion.8, bf16[1,256,7168]{2,1,0:T(8,128)(2,1)S(1)} %copy-done.2), kind=kOutput, calls=%fused_computation.2 | convolution fusion | flops 2824077312 | bytes 15073280 | tf_op jit(solution)/shard_map/hcf,fd->hcd/dot_general | solution.py:47
  133.2 51.3 %copy.51 = bf16[32,24,7168]{1,0,2:T(8,128)(2,1)} copy(bf16[32,24,7168]{2,1,0:T(8,128)(2,1)} %convolution_convert_fusion) | data formatting | bytes 22020096
  184.5 81.1 %reshape.49 = bf16[7168,768]{1,0:T(8,128)(2,1)} reshape(bf16[7168,32,24]{2,1,0:T(8,128)(2,1)} %bitcast.33) | data formatting | bytes 22020096
  265.6 0.0 reduce-scatter.4.cloned.1.call-update
  265.6 68.0 %reduce-scatter.4.cloned.1.call-done = bf16[896,768]{1,0:T(8,128)(2,1)} async-done(((bf16[7168,768]{1,0:T(8,128)(2,1)}), bf16[896,768]{1,0:T(8,128)(2,1)}) %reduce-scatter.4.cloned.1.call-update) | async-done | bytes 1376272
  333.7 13.4 %reshape.50 = bf16[896,32,24]{2,1,0:T(8,128)(2,1)} reshape(bf16[896,768]{1,0:T(8,128)(2,1)} %reduce-scatter.4.cloned.1.call-done) | data formatting | bytes 2752512
  347.0 0.0 copy-start.3
  347.0 9.7 %copy.52 = bf16[32,24,896]{2,1,0:T(8,128)(2,1)} copy(bf16[32,24,896]{1,0,2:T(8,128)(2,1)} %bitcast.35) | data formatting | bytes 2752512
  356.8 10.1 %all-to-all-start.1 = ((bf16[32,24,896]{2,1,0:T(8,128)(2,1)}), bf16[32,24,896]{2,1,0:T(8,128)(2,1)S(1)}, u32[]{:S(2)}, u32[]{:S(2)}) async-start(bf16[32,24,896]{2,1,0:T(8,128)(2,1)} %copy.52), calls=%async_computation.1 | async-start | bytes 2752512 | tf_op jit(solution)/shard_map/all_to_all | solution.py:51
  366.9 0.0 copy-done.3
  366.9 0.1 copy.45
  367.0 0.1 reshape.32
  367.1 0.0 copy-start.4
  367.1 3.8 gather_fusion.1
  370.9 0.1 reshape.35
  371.0 0.1 copy.46
  371.1 0.1 copy.49
  371.2 0.1 reshape.26
  371.3 0.1 copy.47
  371.5 0.0 copy-done.4
  371.5 0.1 copy.50
  371.6 30.0 %all-to-all-done.1 = bf16[32,24,896]{2,1,0:T(8,128)(2,1)S(1)} async-done(((bf16[32,24,896]{2,1,0:T(8,128)(2,1)}), bf16[32,24,896]{2,1,0:T(8,128)(2,1)S(1)}, u32[]{:S(2)}, u32[]{:S(2)}) %all-to-all-start.1) | async-done | bytes 1376288 | tf_op jit(solution)/shard_map/all_to_all | solution.py:51
  401.6 0.0 copy-start.1
  401.6 2.0 gather_fusion
  403.6 0.2 reshape.25
  403.9 2.1 multiply_reduce_fusion
  406.0 0.0 copy-done.1
  (5 shorter events, 0.1 us)
Async XLA Ops:
  6.5 1.1 copy-start
  6.5 108.2 %all-gather.2.cloned.1.call-start = ((), (), s32[]{:S(2)}) async-start(), calls=%async_computation.3 | async-start | bytes 12386304 | tf_op jit(solution)/shard_map/all_gather | solution.py:43
  55.6 278.1 %reduce-scatter.4.cloned.1.call-start = ((), (), s32[]{:S(2)}) async-start(), calls=%async_computation.4 | async-start | bytes 12386304
  114.7 8.4 %copy-start.5 = (bf16[32,24,7168]{2,1,0:T(8,128)(2,1)S(1)}, bf16[32,24,7168]{2,1,0:T(8,128)(2,1)}, u32[]{:S(2)}) copy-start(bf16[32,24,7168]{2,1,0:T(8,128)(2,1)} %all-gather.2.cloned.1.call-done) | copy-start | bytes 33030148
  114.7 9.4 %copy-start.6 = (bf16[1,7168,256]{2,1,0:T(8,128)(2,1)S(1)}, bf16[1,7168,256]{2,1,0:T(8,128)(2,1)}, u32[]{:S(2)}) copy-start(bf16[1,7168,256]{2,1,0:T(8,128)(2,1)} %param.10) | copy-start | bytes 11010052
  124.1 3.2 copy-start.2
  347.0 19.8 %copy-start.3 = (s32[128,4]{0,1:T(4,128)S(1)}, s32[128,4]{0,1:T(4,128)}, u32[]{:S(2)}) copy-start(s32[128,4]{0,1:T(4,128)} %param.7) | copy-start | bytes 6148
  356.8 44.8 %all-to-all-start.1 = ((bf16[32,24,896]{2,1,0:T(8,128)(2,1)}), bf16[32,24,896]{2,1,0:T(8,128)(2,1)S(1)}, u32[]{:S(2)}, u32[]{:S(2)}) async-start(bf16[32,24,896]{2,1,0:T(8,128)(2,1)} %copy.52), calls=%async_computation.1 | async-start | bytes 2752512 | tf_op jit(solution)/shard_map/all_to_all | solution.py:51
  367.1 4.4 %copy-start.4 = (f32[128,4]{0,1:T(4,128)S(1)}, f32[128,4]{0,1:T(4,128)}, u32[]{:S(2)}) copy-start(f32[128,4]{0,1:T(4,128)} %param.8) | copy-start | bytes 6148
  401.6 4.4 %copy-start.1 = (bf16[128,896]{1,0:T(8,128)(2,1)S(1)}, bf16[128,896]{1,0:T(8,128)(2,1)}, u32[]{:S(2)}) copy-start(bf16[128,896]{1,0:T(8,128)(2,1)} %param.6) | copy-start | bytes 688132
Sparse Core Ops, SparseCore 0:
  55.7 58.9 all-gather.1
  265.8 67.8 reduce-scatter.3
where the time goes:
time: 417 us; the launch traced here: 413 us
  local copies, waits for them, and re-layouts  165 us (40%)
  waiting for transfers between devices  157 us (38%)
  blocking collectives  47.4 us (11%)
  matrix products  16.6 us (4%)
  between operations  13.5 us (3%)
  starting transfers between devices  10.1 us (2%)
    unnamed x19, local copies, waits for them, and re-layouts  158 us
    unnamed x3, waiting for transfers between devices  68 us
    all_gather x1, waiting for transfers between devices, local(): feature_part = lax.all_gather(arrived, 'inner', axis=2, tiled=True)  59.1 us
    all_to_all x1, blocking collectives, local(): lax.all_to_all(pack_rows(placing, tokens), 'group', split_axis=0, concat_...  47.4 us
    all_to_all x1, waiting for transfers between devices, local(): lax.all_to_all(summed, 'group', split_axis=0, concat_axis=0, tiled=True)  30 us
    all_to_all x1, starting transfers between devices, local(): lax.all_to_all(summed, 'group', split_axis=0, concat_axis=0, tiled=True)  10.1 us
  transfers between devices with their start and end apart: 3, of which 3 were waited for; matrix products, arithmetic and copies ran while one was open for 1% of the time, Pallas kernels for 0%

commit v1 on v0

--- a/solution.py
+++ b/solution.py
@@ -40,7 +40,9 @@
     arrived = lax.all_to_all(
         pack_rows(placing, tokens), "group", split_axis=0, concat_axis=0, tiled=True
     )
-    feature_part = lax.all_gather(arrived, "inner", axis=2, tiled=True)
+    feature_part = jnp.concatenate(
+        lax.all_to_all(jnp.stack([arrived] * lax.axis_size("inner")), "inner", 0, 0), axis=2
+    )
     gate_add = jnp.einsum("hck,kf->hcf", feature_part, gate_mat, preferred_element_type=jnp.float32)
     up_add = jnp.einsum("hck,kf->hcf", feature_part, up_mat, preferred_element_type=jnp.float32)
     hidden = (jax.nn.silu(gate_add) * up_add).astype(jnp.bfloat16)

time: 417 us -> 481 us (1.15)
  blocking collectives: 47.4 us -> 174 us
  waiting for transfers between devices: 157 us -> 92.6 us
  local copies, waits for them, and re-layouts: 165 us -> 171 us
    all_to_all x0 -> x1, blocking collectives: none -> 127 us  [local(): lax.all_to_all(jnp.stack([arrived] * lax.axis_size('inner')), 'inner', 0, 0)]
    all_gather x1 -> x0, waiting for transfers between devices: 59.1 us -> none  [local(): feature_part = lax.all_gather(arrived, 'inner', axis=2, tiled=True)]
    unnamed x3 -> x2, waiting for transfers between devices: 68 us -> 62.6 us
    another operation x0 -> x1, local copies, waits for them, and re-layouts: none -> 5.01 us  [local(): jnp.stack([arrived] * lax.axis_size('inner'))]
  transfers between devices with their start and end apart: 3 -> 2, of which waited for: 3 -> 2; matrix products, arithmetic and copies ran while one was open for 1% -> 1% of each run, Pallas kernels for 0% -> 0%
where the time goes in v1:
time: 481 us; the launch traced here: 477 us
  blocking collectives  174 us (36%)
  local copies, waits for them, and re-layouts  171 us (36%)
  waiting for transfers between devices  92.6 us (19%)
  between operations  13.6 us (3%)
  matrix products  12.8 us (3%)
  starting transfers between devices  10.1 us (2%)
    unnamed x19, local copies, waits for them, and re-layouts  156 us
    all_to_all x1, blocking collectives, local(): lax.all_to_all(jnp.stack([arrived] * lax.axis_size('inner')), 'inner', 0, 0)  127 us
    unnamed x2, waiting for transfers between devices  62.6 us
    all_to_all x1, blocking collectives, local(): lax.all_to_all(pack_rows(placing, tokens), 'group', split_axis=0, concat_...  47.3 us
    all_to_all x1, waiting for transfers between devices, local(): lax.all_to_all(summed, 'group', split_axis=0, concat_axis=0, tiled=True)  30 us
    all_to_all x1, starting transfers between devices, local(): lax.all_to_all(summed, 'group', split_axis=0, concat_axis=0, tiled=True)  10.1 us
  transfers between devices with their start and end apart: 2, of which 2 were waited for; matrix products, arithmetic and copies ran while one was open for 1% of the time, Pallas kernels for 0%

profile of v1, /device:TPU:32, one launch (start us, length us, event | category | flops | bytes accessed | tf_op | source)
XLA Modules:
  0.0 477.2 jit_solution(18128222939110414743)
XLA Ops:
  6.5 0.0 copy-start
  6.5 0.0 reduce-scatter.4.cloned.1.call-start
  6.5 0.7 convert_reduce_fusion
  7.3 0.1 copy.46
  7.4 0.2 reduce_window_sum.11
  7.6 0.1 copy.50
  7.6 0.0 copy-done
  7.6 0.5 convolution_convert_fusion.1
  8.2 47.3 %all_to_all.15 = bf16[32,24,896]{2,1,0:T(8,128)(2,1)S(1)} all-to-all(bf16[32,24,896]{2,1,0:T(8,128)(2,1)S(1)} %convolution_convert_fusion.1), channel_id=1, replica_groups=mesh['group'=32,'inner'=8] {'group'}, dimensions={0} | all-to-all | bytes 2752512 | tf_op jit(solution)/shard_map/all_to_all | solution.py:40
  55.4 5.0 %stack.2 = bf16[8,32,24,896]{3,2,1,0:T(8,128)(2,1)} broadcast(bf16[32,24,896]{2,1,0:T(8,128)(2,1)S(1)} %all_to_all.15), dimensions={1,2,3} | broadcast | bytes 12386304 | tf_op jit(solution)/shard_map/stack | solution.py:44
  60.5 127.0 %all_to_all.16 = bf16[8,32,24,896]{3,2,1,0:T(8,128)(2,1)S(1)} all-to-all(bf16[8,32,24,896]{3,2,1,0:T(8,128)(2,1)} %stack.2), channel_id=1, replica_groups=mesh['group'=32,'inner'=8] {'inner'}, dimensions={0} | all-to-all | bytes 22020096 | tf_op jit(solution)/shard_map/all_to_all | solution.py:44
  187.5 0.0 copy-start.5
  187.5 3.3 copy.56
  190.8 0.0 copy-done.5
  190.8 0.0 copy-start.6
  190.8 3.2 fusion.3
  194.0 0.0 copy-done.6
  194.0 0.0 copy-start.2
  194.1 3.3 fusion.8
  197.4 0.0 copy-done.2
  197.4 5.7 %convolution_convert_fusion = bf16[32,24,7168]{2,1,0:T(8,128)(2,1)} fusion(bf16[32,24,256]{2,1,0:T(8,128)(2,1)S(1)} %fusion.8, bf16[1,256,7168]{2,1,0:T(8,128)(2,1)S(1)} %copy-done.2), kind=kOutput, calls=%fused_computation.2 | convolution fusion | flops 2824077312 | bytes 15073280 | tf_op jit(solution)/shard_map/hcf,fd->hcd/dot_general | solution.py:49
  203.1 51.2 %copy.54 = bf16[32,24,7168]{1,0,2:T(8,128)(2,1)} copy(bf16[32,24,7168]{2,1,0:T(8,128)(2,1)} %convolution_convert_fusion) | data formatting | bytes 22020096
  254.3 81.1 %reshape.59 = bf16[7168,768]{1,0:T(8,128)(2,1)} reshape(bf16[7168,32,24]{2,1,0:T(8,128)(2,1)} %bitcast.36) | data formatting | bytes 22020096
  335.4 0.0 reduce-scatter.4.cloned.1.call-update
  335.4 62.5 %reduce-scatter.4.cloned.1.call-done = bf16[896,768]{1,0:T(8,128)(2,1)} async-done(((bf16[7168,768]{1,0:T(8,128)(2,1)}), bf16[896,768]{1,0:T(8,128)(2,1)}) %reduce-scatter.4.cloned.1.call-update) | async-done | bytes 1376272
  398.0 13.4 %reshape.60 = bf16[896,32,24]{2,1,0:T(8,128)(2,1)} reshape(bf16[896,768]{1,0:T(8,128)(2,1)} %reduce-scatter.4.cloned.1.call-done) | data formatting | bytes 2752512
  411.4 0.0 copy-start.3
  411.4 9.8 %copy.55 = bf16[32,24,896]{2,1,0:T(8,128)(2,1)} copy(bf16[32,24,896]{1,0,2:T(8,128)(2,1)} %bitcast.39) | data formatting | bytes 2752512
  421.1 10.1 %all-to-all-start.2 = ((bf16[32,24,896]{2,1,0:T(8,128)(2,1)}), bf16[32,24,896]{2,1,0:T(8,128)(2,1)S(1)}, u32[]{:S(2)}, u32[]{:S(2)}) async-start(bf16[32,24,896]{2,1,0:T(8,128)(2,1)} %copy.55), calls=%async_computation.2 | async-start | bytes 2752512 | tf_op jit(solution)/shard_map/all_to_all | solution.py:53
  431.2 0.0 copy-done.3
  431.3 0.1 copy.47
  431.4 0.1 reshape.42
  431.5 0.0 copy-start.4
  431.5 3.8 gather_fusion.1
  435.3 0.1 reshape.45
  435.4 0.1 copy.48
  435.5 0.1 copy.52
  435.6 0.1 reshape.36
  435.7 0.1 copy.49
  435.8 0.0 copy-done.4
  435.8 0.1 copy.53
  436.0 30.0 %all-to-all-done.2 = bf16[32,24,896]{2,1,0:T(8,128)(2,1)S(1)} async-done(((bf16[32,24,896]{2,1,0:T(8,128)(2,1)}), bf16[32,24,896]{2,1,0:T(8,128)(2,1)S(1)}, u32[]{:S(2)}, u32[]{:S(2)}) %all-to-all-start.2) | async-done | bytes 1376288 | tf_op jit(solution)/shard_map/all_to_all | solution.py:53
  466.0 0.0 copy-start.1
  466.0 2.0 gather_fusion
  468.0 0.2 reshape.35
  468.2 2.1 multiply_reduce_fusion
  470.4 0.0 copy-done.1
  (5 shorter events, 0.1 us)
Async XLA Ops:
  6.5 1.1 copy-start
  6.5 391.4 %reduce-scatter.4.cloned.1.call-start = ((), (), s32[]{:S(2)}) async-start(), calls=%async_computation.4 | async-start | bytes 12386304
  187.5 3.3 copy-start.5
  190.8 3.2 copy-start.6
  194.0 3.3 copy-start.2
  411.4 19.9 %copy-start.3 = (s32[128,4]{0,1:T(4,128)S(1)}, s32[128,4]{0,1:T(4,128)}, u32[]{:S(2)}) copy-start(s32[128,4]{0,1:T(4,128)} %param.7) | copy-start | bytes 6148
  421.1 44.8 %all-to-all-start.2 = ((bf16[32,24,896]{2,1,0:T(8,128)(2,1)}), bf16[32,24,896]{2,1,0:T(8,128)(2,1)S(1)}, u32[]{:S(2)}, u32[]{:S(2)}) async-start(bf16[32,24,896]{2,1,0:T(8,128)(2,1)} %copy.55), calls=%async_computation.2 | async-start | bytes 2752512 | tf_op jit(solution)/shard_map/all_to_all | solution.py:53
  431.5 4.4 copy-start.4
  466.0 4.4 copy-start.1
Sparse Core Ops, SparseCore 0:
  335.6 62.3 reduce-scatter.3
